TPU v7x, 32 devices: a whole 2x2x4 slice. The times are simulated.
32 devices in a mesh: row: 8 (over z, x), ch: 4 (over y, core).
Axes of the slice: x: 2, y: 2, z: 4, core: 2. Of those that a mesh axis runs over, the one named last changes fastest.
Arguments:
- pair_rep: bfloat16 [128, 8, 8], P('ch', 'row'), may hold values from -6 to 6
- residue_mask: int32 [8], replicated, may hold values 0 or 1
- chain_ids: int32 [8], replicated, may hold values from 0 to 3, never falling along the last dimension, each value on 1 to 4 neighbouring positions
- in_gain: float32 [2, 128], replicated, may hold values from 0.5 to 1.5
- in_bias: float32 [2, 128], replicated, may hold values from -3 to 3
- w_proj: bfloat16 [2, 128, 4, 128], P(None, None, None, 'ch'), may hold values from -0.5 to 0.5
- w_gate: bfloat16 [2, 128, 128], P(None, None, 'ch'), may hold values from -0.5 to 0.5
- pair_bias: float32 [2, 128], P(None, 'ch'), may hold values from -4 to 4
- out_gain: float32 [2, 128], P(None, 'ch'), may hold values from 0.5 to 1.5
- out_bias: float32 [2, 128], P(None, 'ch'), may hold values from -3 to 3
- w_out: bfloat16 [2, 128, 128], P(None, 'ch'), may hold values from -0.5 to 0.5
Outputs:
- pair_out: bfloat16 [128, 8, 8], P('ch', 'row')
Inputs may be any that keep to these rules, and one draw needn't show every extreme that they name: `chain_ids`: chain numbers never fall along the residues; each chain has 1 to 4 residues.
All inputs are finite; a program needn't handle non-finite values.
Results may differ from a plain program's by a relative error of at most 0.013.
Values may be sent and summed in bfloat16 or wider, within the bound.
A program may use at most 64 MiB of HBM per device.

v0:
```python
import functools
import jax
import jax.numpy as jnp
from jax import lax
from jax.experimental import pallas as pl
from jax.experimental.pallas import tpu as pltpu
from jax.sharding import PartitionSpec as P

epsilon = 1e-05
MESH = pl.DeviceIdType.MESH
F32 = jnp.float32
BF16 = jnp.bfloat16


def lane_norm(values, gain, bias):
    mean_val = jnp.mean(values, axis=-1, keepdims=True)
    variance = jnp.mean(values * values, axis=-1, keepdims=True) - mean_val * mean_val
    return ((values - mean_val) * lax.rsqrt(variance + epsilon) * gain + bias).astype(BF16)


def dot_nt(a, b):
    return lax.dot_general(a, b, (((1,), (1,)), ((), ())), preferred_element_type=F32)


def dot_nn(a, b):
    return lax.dot_general(a, b, (((1,), (0,)), ((), ())), preferred_element_type=F32)


def window_kernel(
    rows,
    chs,
    mask_ref,
    chain_ref,
    pair_ref,
    in_gain_ref,
    in_bias_ref,
    proj_ref,
    gate_ref,
    bias_ref,
    gain_ref,
    offset_ref,
    mix_ref,
    out_ref,
    block_buf,
    proj_buf,
    gate_buf,
    mix_buf,
    vector_buf,
    pair_buf,
    left_buf,
    right_buf,
    middle_buf,
    normed_buf,
    block_send,
    block_recv,
    vector_send,
    vector_recv,
    weight_send,
    weight_recv,
    row_send,
    row_recv,
    own_sem,
):
    n = pair_buf.shape[0]
    lanes = pair_buf.shape[2]
    block = lanes // chs
    row = lax.axis_index("row")
    ch = lax.axis_index("ch")

    barrier = pltpu.get_barrier_semaphore()
    for step in range(1, chs):
        pl.semaphore_signal(
            barrier, inc=1, device_id=(row, lax.rem(ch + step, chs)), device_id_type=MESH
        )
    for step in range(1, rows):
        pl.semaphore_signal(
            barrier, inc=1, device_id=(lax.rem(row + step, rows), ch), device_id_type=MESH
        )

    first = [(pair_ref, block_buf.at[ch], 0, block_send, block_recv)]
    vectors_out = [
        (ref, vector_buf.at[t, ch], 1 + t, vector_send.at[t], vector_recv.at[t])
        for t, ref in enumerate((bias_ref, gain_ref, offset_ref))
    ]
    weights_out = []
    for u in range(2):
        group = []
        for t, (ref, buf) in enumerate(
            ((proj_ref, proj_buf), (gate_ref, gate_buf), (mix_ref, mix_buf))
        ):
            group.append(
                (
                    ref.at[u],
                    buf.at[u, ch],
                    4 + 3 * u + t,
                    weight_send.at[u, t],
                    weight_recv.at[u, t],
                )
            )
        weights_out.append(group)

    def keep(items):
        copies = [pltpu.make_async_copy(src, dst, own_sem.at[k]) for src, dst, k, _, _ in items]
        for copy in copies:
            copy.start()
        return copies

    def spread(items):
        copies = []
        for src, dst, _, send, recv in items:
            for step in range(1, chs):
                copy = pltpu.make_async_remote_copy(
                    src_ref=src,
                    dst_ref=dst,
                    send_sem=send.at[step - 1],
                    recv_sem=recv.at[step - 1],
                    device_id=(row, lax.rem(ch + step, chs)),
                    device_id_type=MESH,
                )
                copy.start()
                copies.append(copy)
        return copies

    def arrive(own, remote):
        for copy in own:
            copy.wait()
        for copy in remote:
            copy.wait_recv()

    own_first = keep(first)
    own_weights = [keep(weights_out[0] + vectors_out), keep(weights_out[1])]

    place = lax.broadcasted_iota(jnp.int32, (n, lanes), 0)
    mask_j = jnp.zeros((n, lanes), jnp.int32)
    chain_j = jnp.zeros((n, lanes), jnp.int32)
    for j in range(n):
        mask_j = jnp.where(place == j, mask_ref[j], mask_j)
        chain_j = jnp.where(place == j, chain_ref[j], chain_j)
    pair_mask = jnp.concatenate([(mask_j * mask_ref[i]).astype(F32) for i in range(n)], axis=0)
    same_chain = jnp.concatenate(
        [jnp.where(chain_j == chain_ref[i], 1.0, 0.0).astype(F32) for i in range(n)], axis=0
    )
    same_here = jnp.where(chain_j == chain_ref[row], 1.0, 0.0).astype(F32)

    pl.semaphore_wait(barrier, chs - 1 + rows - 1)
    remote_first = spread(first)
    remote_weights = [spread(weights_out[0] + vectors_out), spread(weights_out[1])]

    arrive(own_first, remote_first)
    pair_buf[row] = jnp.concatenate([block_buf[m].astype(F32) for m in range(chs)], axis=1)
    row_copies = []
    for step in range(1, rows):
        copy = pltpu.make_async_remote_copy(
            src_ref=pair_buf.at[row],
            dst_ref=pair_buf.at[row],
            send_sem=row_send.at[step - 1],
            recv_sem=row_recv.at[step - 1],
            device_id=(lax.rem(row + step, rows), ch),
            device_id_type=MESH,
        )
        copy.start()
        row_copies.append(copy)

    def projection(u, part):
        here = slice(part * block, (part + 1) * block)
        return proj_buf[u, :, here, :].reshape(lanes, lanes)

    def vector(t, u):
        return jnp.concatenate([vector_buf[t, m, u : u + 1, :] for m in range(chs)], axis=1)

    def arms(u, normed):
        left = jax.nn.sigmoid(dot_nt(normed, projection(u, 0))) * dot_nt(normed, projection(u, 1))
        right = jax.nn.sigmoid(dot_nt(normed, projection(u, 2))) * dot_nt(normed, projection(u, 3))
        left_buf[...] = (left * pair_mask).astype(BF16).astype(F32)
        right_buf[...] = (right * pair_mask).astype(BF16).astype(F32)

    def update(u, pair, normed, product, same):
        xn = lane_norm(product, vector(1, u), vector(2, u))
        mixed = dot_nn(xn, mix_buf[u].reshape(lanes, lanes))
        logits = dot_nt(normed, gate_buf[u].reshape(lanes, lanes)) + vector(0, u) * same
        return (pair + jax.nn.sigmoid(logits) * mixed).astype(BF16)

    arrive([], row_copies)
    pair = pair_buf[...].reshape(n * n, lanes)
    normed = lane_norm(pair, in_gain_ref[0:1, :], in_bias_ref[0:1, :])
    arrive(own_weights[0], remote_weights[0])
    arms(0, normed)
    right_k = [right_buf[pl.ds(k, n, stride=n), :] for k in range(n)]
    product = []
    for i in range(n):
        total = left_buf[i * n : i * n + 1, :] * right_k[0]
        for k in range(1, n):
            total = total + left_buf[i * n + k : i * n + k + 1, :] * right_k[k]
        product.append(total)
    middle = update(0, pair, normed, jnp.concatenate(product, axis=0), same_chain).astype(F32)
    middle_buf[...] = middle

    normed = lane_norm(middle, in_gain_ref[1:2, :], in_bias_ref[1:2, :])
    normed_buf[...] = normed.astype(F32)
    arrive(own_weights[1], remote_weights[1])
    arms(1, normed)
    total = left_buf[pl.ds(row, 1), :] * right_buf[0:n, :]
    for k in range(1, n):
        total = total + left_buf[pl.ds(k * n + row, 1), :] * right_buf[k * n : (k + 1) * n, :]
    here = pl.ds(pl.multiple_of(row * n, n), n)
    result = update(1, middle_buf[here, :], normed_buf[here, :].astype(BF16), total, same_here)

    picked = lax.broadcasted_iota(jnp.int32, (block, lanes), 1)
    wanted = lax.broadcasted_iota(jnp.int32, (block, lanes), 0) + ch * block
    chosen = jnp.where(picked == wanted, 1.0, 0.0).astype(BF16)
    out_ref[...] = dot_nt(result, chosen).astype(BF16)

    for copy in remote_first + remote_weights[0] + remote_weights[1] + row_copies:
        copy.wait_send()


def window_body(
    rows,
    chs,
    pair_rep,
    residue_mask,
    chain_ids,
    in_gain,
    in_bias,
    w_proj,
    w_gate,
    pair_bias,
    out_gain,
    out_bias,
    w_out,
):
    block, _, n = pair_rep.shape
    lanes = in_gain.shape[1]
    layers, _, parts, _ = w_proj.shape
    vmem = pl.BlockSpec(memory_space=pltpu.VMEM)
    smem = pl.BlockSpec(memory_space=pltpu.SMEM)
    dma = pltpu.SemaphoreType.DMA
    out = pl.pallas_call(
        functools.partial(window_kernel, rows, chs),
        out_shape=jax.ShapeDtypeStruct((n, block), BF16),
        in_specs=[smem, smem] + [vmem] * 9,
        out_specs=vmem,
        scratch_shapes=[
            pltpu.VMEM((chs, n, block), BF16),
            pltpu.VMEM((layers, chs, parts * block, lanes), BF16),
            pltpu.VMEM((layers, chs, block, lanes), BF16),
            pltpu.VMEM((layers, chs, block, lanes), BF16),
            pltpu.VMEM((3, chs, layers, block), F32),
            pltpu.VMEM((n, n, lanes), F32),
            pltpu.VMEM((n * n, lanes), F32),
            pltpu.VMEM((n * n, lanes), F32),
            pltpu.VMEM((n * n, lanes), F32),
            pltpu.VMEM((n * n, lanes), F32),
            dma((chs - 1,)),
            dma((chs - 1,)),
            dma((3, chs - 1)),
            dma((3, chs - 1)),
            dma((layers, 3, chs - 1)),
            dma((layers, 3, chs - 1)),
            dma((rows - 1,)),
            dma((rows - 1,)),
            dma((4 + 3 * layers,)),
        ],
        compiler_params=pltpu.CompilerParams(collective_id=0, has_side_effects=True),
    )(
        residue_mask,
        chain_ids,
        jnp.swapaxes(pair_rep[:, 0, :], 0, 1),
        in_gain,
        in_bias,
        jnp.transpose(w_proj, (0, 2, 3, 1)).reshape(layers, parts * block, lanes),
        jnp.swapaxes(w_gate, 1, 2),
        pair_bias,
        out_gain,
        out_bias,
        w_out,
    )
    return jnp.swapaxes(out, 0, 1)[:, None, :]


def channel_norm(values, norm_gain, norm_bias):
    mean_val = jnp.mean(values, axis=0)
    variance = jnp.mean(values * values, axis=0) - mean_val * mean_val
    return (values - mean_val) * lax.rsqrt(variance + epsilon) * norm_gain[
        :, None, None
    ] + norm_bias[:, None, None]


def prepare(
    pair_local, layer, in_gain, in_bias, w_proj, w_gate, pair_bias, mask_rows, mask_cols, same_chain
):
    full_pair = lax.all_gather(pair_local, "ch", axis=0, tiled=True)
    normed = channel_norm(full_pair.astype(jnp.float32), in_gain[layer], in_bias[layer]).astype(
        jnp.bfloat16
    )
    projected = jnp.einsum(
        "cij,cpd->pdij", normed, w_proj[layer], preferred_element_type=jnp.float32
    )
    pair_mask = mask_rows[:, None] * mask_cols[None, :]
    first_arm = (jax.nn.sigmoid(projected[0]) * projected[1] * pair_mask).astype(jnp.bfloat16)
    second_arm = (jax.nn.sigmoid(projected[2]) * projected[3] * pair_mask).astype(jnp.bfloat16)
    logits = jnp.einsum("cij,cd->dij", normed, w_gate[layer], preferred_element_type=jnp.float32)
    logits = logits + pair_bias[layer][:, None, None] * same_chain[None]
    return (first_arm, second_arm, jax.nn.sigmoid(logits))


def finish(product_sum, gating, layer, out_gain, out_bias, w_out):
    totals = lax.psum(
        (jnp.sum(product_sum, axis=0), jnp.sum(product_sum * product_sum, axis=0)), "ch"
    )
    channels = product_sum.shape[0] * lax.axis_size("ch")
    mean_val = totals[0] / channels
    variance = totals[1] / channels - mean_val * mean_val
    scaled = (product_sum - mean_val) * lax.rsqrt(variance + epsilon)
    normed = (scaled * out_gain[layer][:, None, None] + out_bias[layer][:, None, None]).astype(
        jnp.bfloat16
    )
    columns = w_out[layer]
    mixed = lax.psum_scatter(
        jnp.einsum("dij,dc->cij", normed, columns, preferred_element_type=jnp.float32).astype(
            jnp.bfloat16
        ),
        "ch",
        scatter_dimension=0,
        tiled=True,
    ).astype(jnp.float32)
    return gating * mixed


def body(
    pair_rep,
    residue_mask,
    chain_ids,
    in_gain,
    in_bias,
    w_proj,
    w_gate,
    pair_bias,
    out_gain,
    out_bias,
    w_out,
):
    rows_here = pair_rep.shape[1]
    row_start = lax.axis_index("row") * rows_here
    mask_cols = residue_mask.astype(jnp.float32)
    mask_rows = lax.dynamic_slice_in_dim(mask_cols, row_start, rows_here)
    chain_rows = lax.dynamic_slice_in_dim(chain_ids, row_start, rows_here)
    same_chain = (chain_rows[:, None] == chain_ids[None, :]).astype(jnp.float32)
    first_arm, second_arm, gating = prepare(
        pair_rep, 0, in_gain, in_bias, w_proj, w_gate, pair_bias, mask_rows, mask_cols, same_chain
    )
    product_sum = jnp.einsum(
        "cik,cjk->cij",
        first_arm,
        lax.all_gather(second_arm, "row", axis=1, tiled=True),
        preferred_element_type=jnp.float32,
    )
    middle = (
        pair_rep.astype(jnp.float32) + finish(product_sum, gating, 0, out_gain, out_bias, w_out)
    ).astype(jnp.bfloat16)
    in_first, in_second, in_gating = prepare(
        middle, 1, in_gain, in_bias, w_proj, w_gate, pair_bias, mask_rows, mask_cols, same_chain
    )
    exchanged_left = lax.all_to_all(in_first, "row", split_axis=2, concat_axis=1, tiled=True)
    left_rows = jnp.swapaxes(exchanged_left, 1, 2)
    in_product = jnp.einsum(
        "cik,ckj->cij",
        left_rows,
        lax.all_gather(in_second, "row", axis=1, tiled=True),
        preferred_element_type=jnp.float32,
    )
    update = finish(in_product, in_gating, 1, out_gain, out_bias, w_out)
    return (middle.astype(jnp.float32) + update).astype(jnp.bfloat16)


def choose(rows, chs, *args):
    pair_rep, in_gain = args[0], args[3]
    n, lanes = pair_rep.shape[2], in_gain.shape[1]
    one_tile = pair_rep.shape[1] == 1 and n == rows == 8 and lanes == 128
    if one_tile and chs > 1 and args[5].shape[1] == pair_rep.shape[0] * chs:
        return window_body(rows, chs, *args)
    return body(*args)


def solution(mesh):
    return jax.shard_map(
        functools.partial(choose, mesh.shape["row"], mesh.shape["ch"]),
        mesh=mesh,
        in_specs=(
            P("ch", "row", None),
            P(),
            P(),
            P(),
            P(),
            P(None, None, None, "ch"),
            P(None, None, "ch"),
            P(None, "ch"),
            P(None, "ch"),
            P(None, "ch"),
            P(None, "ch", None),
        ),
        out_specs=P("ch", "row", None),
        check_vma=False,
    )
```

profile of v0, /device:TPU:0, one launch (start us, length us, event | category | flops | bytes accessed | tf_op | source)
XLA Modules:
  0.0 16.5 jit_solution(8755897363414991142)
XLA Ops:
  0.0 15.2 %shard_map.109 = bf16[8,32]{1,0:T(8,128)(2,1)} custom-call(s32[8]{0:T(128)} %mask_ref.1, s32[8]{0:T(128)} %chain_ref.1, bf16[8,32]{1,0:T(8,128)(2,1)} %bitcast.13, f32[2,128]{1,0:T(2,128)} %in_gain_ref.1, f32[2,128]{1,0:T(2,128)} %in_bias_ref.1, bf16[2,128,128]{2,1,0:T(8,128)(2,1)} %bitcast.10, bf16[2,32,128]{2,1,0:T(8,128)(2,1)} %bitcast.11, ...), custom_call_target="tpu_custom_call" | custom-call | tf_op jit(solution)/shard_map/pallas_call | solution.py:238
  15.2 1.3 %copy.13 = bf16[32,1,8]{0,2,1:T(8,128)(2,1)} copy(bf16[32,1,8]{0,2,1:T(8,128)(2,1)} %bitcast.12) | data formatting | bytes 1024
where the time goes:
time: 16.7 us; the launch traced here: 16.5 us
  Pallas kernels  15.2 us (91%)
  local copies, waits for them, and re-layouts  1.26 us (8%)
    pallas_call x1, Pallas kernels, window_body(): pl.pallas_call(functools.partial(window_kernel, rows, chs), out_shape=jax...  15.2 us
    unnamed x1, local copies, waits for them, and re-layouts  1.26 us

commit v1 on v0

--- a/solution.py
+++ b/solution.py
@@ -26,110 +26,122 @@
     return lax.dot_general(a, b, (((1,), (0,)), ((), ())), preferred_element_type=F32)
 
 
+def drain(ref, sem):
+    pltpu.make_async_copy(ref, ref, sem).wait()
+
+
 def window_kernel(
     rows,
     chs,
+    mask_hbm,
+    chain_hbm,
+    pair_hbm,
+    in_gain_hbm,
+    in_bias_hbm,
+    proj_hbm,
+    gate_hbm,
+    bias_hbm,
+    gain_hbm,
+    offset_hbm,
+    mix_hbm,
+    out_ref,
     mask_ref,
     chain_ref,
-    pair_ref,
-    in_gain_ref,
-    in_bias_ref,
-    proj_ref,
-    gate_ref,
-    bias_ref,
-    gain_ref,
-    offset_ref,
-    mix_ref,
-    out_ref,
+    norm_buf,
     block_buf,
     proj_buf,
     gate_buf,
     mix_buf,
     vector_buf,
-    pair_buf,
     left_buf,
     right_buf,
     middle_buf,
     normed_buf,
+    ready_sem,
+    scalar_sem,
+    norm_sem,
     block_send,
     block_recv,
     vector_send,
     vector_recv,
     weight_send,
     weight_recv,
-    row_send,
-    row_recv,
-    own_sem,
 ):
-    n = pair_buf.shape[0]
-    lanes = pair_buf.shape[2]
+    n = out_ref.shape[0]
+    lanes = norm_buf.shape[2]
     block = lanes // chs
     row = lax.axis_index("row")
     ch = lax.axis_index("ch")
+    peers = [lax.rem(ch + step, chs) for step in range(1, chs)]
 
     barrier = pltpu.get_barrier_semaphore()
-    for step in range(1, chs):
-        pl.semaphore_signal(
-            barrier, inc=1, device_id=(row, lax.rem(ch + step, chs)), device_id_type=MESH
-        )
-    for step in range(1, rows):
-        pl.semaphore_signal(
-            barrier, inc=1, device_id=(lax.rem(row + step, rows), ch), device_id_type=MESH
-        )
-
-    first = [(pair_ref, block_buf.at[ch], 0, block_send, block_recv)]
-    vectors_out = [
-        (ref, vector_buf.at[t, ch], 1 + t, vector_send.at[t], vector_recv.at[t])
-        for t, ref in enumerate((bias_ref, gain_ref, offset_ref))
+    for peer in peers:
+        pl.semaphore_signal(barrier, inc=1, device_id=(row, peer), device_id_type=MESH)
+
+    @pl.loop(row + 1, rows)
+    def _(other):
+        for m in range(chs):
+            pl.semaphore_signal(barrier, inc=1, device_id=(other, m), device_id_type=MESH)
+
+    pltpu.make_async_copy(mask_hbm, mask_ref, scalar_sem.at[0]).start()
+    pltpu.make_async_copy(chain_hbm, chain_ref, scalar_sem.at[1]).start()
+    pltpu.make_async_copy(in_gain_hbm, norm_buf.at[0], norm_sem.at[0]).start()
+    pltpu.make_async_copy(in_bias_hbm, norm_buf.at[1], norm_sem.at[1]).start()
+    here = row * chs + ch
+    pltpu.make_async_copy(pair_hbm, block_buf.at[here], block_recv).start()
+    vectors = [
+        (ref, vector_buf.at[t, ch], vector_send.at[t], vector_recv.at[t])
+        for t, ref in enumerate((bias_hbm, gain_hbm, offset_hbm))
     ]
-    weights_out = []
-    for u in range(2):
-        group = []
-        for t, (ref, buf) in enumerate(
-            ((proj_ref, proj_buf), (gate_ref, gate_buf), (mix_ref, mix_buf))
-        ):
-            group.append(
-                (
-                    ref.at[u],
-                    buf.at[u, ch],
-                    4 + 3 * u + t,
-                    weight_send.at[u, t],
-                    weight_recv.at[u, t],
-                )
+    weights = [
+        [
+            (ref.at[u], buf.at[u, ch], weight_send.at[u, t], weight_recv.at[u, t])
+            for t, (ref, buf) in enumerate(
+                ((proj_hbm, proj_buf), (gate_hbm, gate_buf), (mix_hbm, mix_buf))
             )
-        weights_out.append(group)
-
-    def keep(items):
-        copies = [pltpu.make_async_copy(src, dst, own_sem.at[k]) for src, dst, k, _, _ in items]
-        for copy in copies:
-            copy.start()
-        return copies
-
-    def spread(items):
-        copies = []
-        for src, dst, _, send, recv in items:
-            for step in range(1, chs):
-                copy = pltpu.make_async_remote_copy(
-                    src_ref=src,
-                    dst_ref=dst,
-                    send_sem=send.at[step - 1],
-                    recv_sem=recv.at[step - 1],
-                    device_id=(row, lax.rem(ch + step, chs)),
-                    device_id_type=MESH,
-                )
-                copy.start()
-                copies.append(copy)
-        return copies
-
-    def arrive(own, remote):
-        for copy in own:
-            copy.wait()
-        for copy in remote:
-            copy.wait_recv()
-
-    own_first = keep(first)
-    own_weights = [keep(weights_out[0] + vectors_out), keep(weights_out[1])]
-
+        ]
+        for u in range(2)
+    ]
+    for src, dst, _, recv in weights[0] + vectors + weights[1]:
+        pltpu.make_async_copy(src, dst, recv).start()
+
+    def send(src, dst, send_sem, recv_sem, r, c):
+        pltpu.make_async_remote_copy(
+            src_ref=src,
+            dst_ref=dst,
+            send_sem=send_sem,
+            recv_sem=recv_sem,
+            device_id=(r, c),
+            device_id_type=MESH,
+        ).start()
+
+    def send_block(r, c):
+        send(pair_hbm, block_buf.at[here], block_send, block_recv, r, c)
+
+    pl.semaphore_wait(barrier, chs - 1 + row * chs)
+
+    @pl.loop(0, row)
+    def _(other):
+        for m in range(chs):
+            send_block(other, m)
+            pl.semaphore_signal(
+                ready_sem.at[row], inc=1, device_id=(other, m), device_id_type=MESH
+            )
+
+    for peer in peers:
+        send_block(row, peer)
+    for src, dst, send_sem, recv_sem in weights[0] + vectors + weights[1]:
+        for peer in peers:
+            send(src, dst, send_sem, recv_sem, row, peer)
+
+    @pl.loop(row + 1, rows)
+    def _(other):
+        pl.semaphore_wait(ready_sem.at[other], chs)
+        for m in range(chs):
+            send_block(other, m)
+
+    drain(mask_hbm, scalar_sem.at[0])
+    drain(chain_hbm, scalar_sem.at[1])
     place = lax.broadcasted_iota(jnp.int32, (n, lanes), 0)
     mask_j = jnp.zeros((n, lanes), jnp.int32)
     chain_j = jnp.zeros((n, lanes), jnp.int32)
@@ -142,28 +154,9 @@
     )
     same_here = jnp.where(chain_j == chain_ref[row], 1.0, 0.0).astype(F32)
 
-    pl.semaphore_wait(barrier, chs - 1 + rows - 1)
-    remote_first = spread(first)
-    remote_weights = [spread(weights_out[0] + vectors_out), spread(weights_out[1])]
-
-    arrive(own_first, remote_first)
-    pair_buf[row] = jnp.concatenate([block_buf[m].astype(F32) for m in range(chs)], axis=1)
-    row_copies = []
-    for step in range(1, rows):
-        copy = pltpu.make_async_remote_copy(
-            src_ref=pair_buf.at[row],
-            dst_ref=pair_buf.at[row],
-            send_sem=row_send.at[step - 1],
-            recv_sem=row_recv.at[step - 1],
-            device_id=(lax.rem(row + step, rows), ch),
-            device_id_type=MESH,
-        )
-        copy.start()
-        row_copies.append(copy)
-
     def projection(u, part):
-        here = slice(part * block, (part + 1) * block)
-        return proj_buf[u, :, here, :].reshape(lanes, lanes)
+        part_rows = slice(part * block, (part + 1) * block)
+        return proj_buf[u, :, part_rows, :].reshape(lanes, lanes)
 
     def vector(t, u):
         return jnp.concatenate([vector_buf[t, m, u : u + 1, :] for m in range(chs)], axis=1)
@@ -180,10 +173,27 @@
         logits = dot_nt(normed, gate_buf[u].reshape(lanes, lanes)) + vector(0, u) * same
         return (pair + jax.nn.sigmoid(logits) * mixed).astype(BF16)
 
-    arrive([], row_copies)
-    pair = pair_buf[...].reshape(n * n, lanes)
-    normed = lane_norm(pair, in_gain_ref[0:1, :], in_bias_ref[0:1, :])
-    arrive(own_weights[0], remote_weights[0])
+    def normalize(u, pair):
+        return lane_norm(pair, norm_buf[0, u : u + 1, :], norm_buf[1, u : u + 1, :])
+
+    def arrive(u):
+        for t, buf in enumerate((proj_buf, gate_buf, mix_buf)):
+            drain(buf.at[u], weight_recv.at[u, t])
+
+    drain(norm_buf.at[0], norm_sem.at[0])
+    drain(norm_buf.at[1], norm_sem.at[1])
+    for t in range(3):
+        drain(vector_buf.at[t], vector_recv.at[t])
+    arrive(0)
+    drain(block_buf, block_recv)
+    pair = jnp.concatenate(
+        [
+            jnp.concatenate([block_buf[i * chs + m].astype(F32) for m in range(chs)], axis=1)
+            for i in range(n)
+        ],
+        axis=0,
+    )
+    normed = normalize(0, pair)
     arms(0, normed)
     right_k = [right_buf[pl.ds(k, n, stride=n), :] for k in range(n)]
     product = []
@@ -195,23 +205,27 @@
     middle = update(0, pair, normed, jnp.concatenate(product, axis=0), same_chain).astype(F32)
     middle_buf[...] = middle
 
-    normed = lane_norm(middle, in_gain_ref[1:2, :], in_bias_ref[1:2, :])
+    normed = normalize(1, middle)
     normed_buf[...] = normed.astype(F32)
-    arrive(own_weights[1], remote_weights[1])
+    arrive(1)
     arms(1, normed)
     total = left_buf[pl.ds(row, 1), :] * right_buf[0:n, :]
     for k in range(1, n):
         total = total + left_buf[pl.ds(k * n + row, 1), :] * right_buf[k * n : (k + 1) * n, :]
-    here = pl.ds(pl.multiple_of(row * n, n), n)
-    result = update(1, middle_buf[here, :], normed_buf[here, :].astype(BF16), total, same_here)
+    mine = pl.ds(pl.multiple_of(row * n, n), n)
+    result = update(1, middle_buf[mine, :], normed_buf[mine, :].astype(BF16), total, same_here)
 
     picked = lax.broadcasted_iota(jnp.int32, (block, lanes), 1)
     wanted = lax.broadcasted_iota(jnp.int32, (block, lanes), 0) + ch * block
     chosen = jnp.where(picked == wanted, 1.0, 0.0).astype(BF16)
     out_ref[...] = dot_nt(result, chosen).astype(BF16)
 
-    for copy in remote_first + remote_weights[0] + remote_weights[1] + row_copies:
-        copy.wait_send()
+    drain(block_buf.at[pl.ds(0, rows * chs - 1)], block_send)
+    for t in range(3):
+        drain(vector_buf.at[t, pl.ds(0, chs - 1)], vector_send.at[t])
+    for u in range(2):
+        for t, buf in enumerate((proj_buf, gate_buf, mix_buf)):
+            drain(buf.at[u, pl.ds(0, chs - 1)], weight_send.at[u, t])
 
 
 def window_body(
@@ -233,33 +247,35 @@
     lanes = in_gain.shape[1]
     layers, _, parts, _ = w_proj.shape
     vmem = pl.BlockSpec(memory_space=pltpu.VMEM)
-    smem = pl.BlockSpec(memory_space=pltpu.SMEM)
+    hbm = pl.BlockSpec(memory_space=pl.ANY)
     dma = pltpu.SemaphoreType.DMA
     out = pl.pallas_call(
         functools.partial(window_kernel, rows, chs),
-        out_shape=jax.ShapeDtypeStruct((n, block), BF16),
-        in_specs=[smem, smem] + [vmem] * 9,
+        out_shape=pltpu.VMEM((n, block), BF16),
+        in_specs=[hbm] * 11,
         out_specs=vmem,
         scratch_shapes=[
-            pltpu.VMEM((chs, n, block), BF16),
+            pltpu.SMEM(residue_mask.shape, jnp.int32),
+            pltpu.SMEM(chain_ids.shape, jnp.int32),
+            pltpu.VMEM((2, layers, lanes), F32),
+            pltpu.VMEM((rows * chs, n, block), BF16),
             pltpu.VMEM((layers, chs, parts * block, lanes), BF16),
             pltpu.VMEM((layers, chs, block, lanes), BF16),
             pltpu.VMEM((layers, chs, block, lanes), BF16),
             pltpu.VMEM((3, chs, layers, block), F32),
-            pltpu.VMEM((n, n, lanes), F32),
             pltpu.VMEM((n * n, lanes), F32),
             pltpu.VMEM((n * n, lanes), F32),
             pltpu.VMEM((n * n, lanes), F32),
             pltpu.VMEM((n * n, lanes), F32),
-            dma((chs - 1,)),
-            dma((chs - 1,)),
-            dma((3, chs - 1)),
-            dma((3, chs - 1)),
-            dma((layers, 3, chs - 1)),
-            dma((layers, 3, chs - 1)),
-            dma((rows - 1,)),
-            dma((rows - 1,)),
-            dma((4 + 3 * layers,)),
+            pltpu.SemaphoreType.REGULAR((rows,)),
+            dma((2,)),
+            dma((2,)),
+            dma,
+            dma,
+            dma((3,)),
+            dma((3,)),
+            dma((layers, 3)),
+            dma((layers, 3)),
         ],
         compiler_params=pltpu.CompilerParams(collective_id=0, has_side_effects=True),
     )(

time: 16.7 us -> 12.3 us (0.74)
  the two profiles are of different devices: /device:TPU:0 before, /device:TPU:25 now
where the time goes in v1:
time: 12.3 us; the launch traced here: 12.2 us
  Pallas kernels  11.6 us (94%)
  local copies, waits for them, and re-layouts  0.58 us (5%)
    pallas_call x1, Pallas kernels, window_body(): pl.pallas_call(functools.partial(window_kernel, rows, chs), out_shape=plt...  11.6 us
    unnamed x1, local copies, waits for them, and re-layouts  0.58 us

profile of v1, /device:TPU:25, one launch (start us, length us, event | category | flops | bytes accessed | tf_op | source)
XLA Modules:
  0.0 12.2 jit_solution(2967986903043148370)
XLA Ops:
  0.0 11.6 %shard_map.109 = bf16[8,32]{1,0:T(8,128)(2,1)S(1)} custom-call(s32[8]{0:T(128)} %mask_hbm.1, s32[8]{0:T(128)} %chain_hbm.1, bf16[8,32]{1,0:T(8,128)(2,1)} %bitcast.13, f32[2,128]{1,0:T(2,128)} %in_gain_hbm.1, f32[2,128]{1,0:T(2,128)} %in_bias_hbm.1, bf16[2,128,128]{2,1,0:T(8,128)(2,1)} %bitcast.11, bf16[2,32,128]{2,1,0:T(8,128)(2,1)} %bitcast.12, ...), custom_call_target="tpu_custom_call" | custom-call | tf_op jit(solution)/shard_map/pallas_call | solution.py:252
  11.6 0.6 %copy.13 = bf16[32,1,8]{0,2,1:T(8,128)(2,1)} copy(bf16[32,1,8]{0,2,1:T(8,128)(2,1)S(1)} %bitcast.10) | data formatting | bytes 1024

commit v2 on v1

--- a/solution.py
+++ b/solution.py
@@ -48,62 +48,106 @@
     mask_ref,
     chain_ref,
     norm_buf,
+    own_buf,
     block_buf,
-    proj_buf,
-    gate_buf,
-    mix_buf,
+    first_buf,
+    second_buf,
+    last_gate_buf,
     vector_buf,
     left_buf,
     right_buf,
     middle_buf,
     normed_buf,
+    near_sem,
     ready_sem,
     scalar_sem,
     norm_sem,
+    own_sem,
     block_send,
     block_recv,
     vector_send,
-    vector_recv,
     weight_send,
-    weight_recv,
+    parcel_recv,
+    far_recv,
+    gate_sem,
 ):
     n = out_ref.shape[0]
     lanes = norm_buf.shape[2]
     block = lanes // chs
+    depth = proj_hbm.shape[1]
     row = lax.axis_index("row")
     ch = lax.axis_index("ch")
-    peers = [lax.rem(ch + step, chs) for step in range(1, chs)]
+    here = row * chs + ch
+
+    last = rows - 1
+    cores = 2
+    partner = ch + 1 - 2 * lax.rem(ch, cores)
+    far = [lax.rem(ch + cores * step, chs) for step in range(1, chs // cores)]
+    mates = far + [partner]
+    is_last = here == rows * chs - 1
 
     barrier = pltpu.get_barrier_semaphore()
-    for peer in peers:
-        pl.semaphore_signal(barrier, inc=1, device_id=(row, peer), device_id_type=MESH)
-
-    @pl.loop(row + 1, rows)
-    def _(other):
-        for m in range(chs):
-            pl.semaphore_signal(barrier, inc=1, device_id=(other, m), device_id_type=MESH)
-
+
+    def greet(r, c):
+        pl.semaphore_signal(barrier, inc=1, device_id=(r, c), device_id_type=MESH)
+
+    @pl.when(jnp.logical_not(is_last))
+    def _():
+        greet(last, chs - 1)
+
+    @pl.when(here < cores)
+    def _():
+        for m in reversed(range(chs - 1)):
+            greet(last, m)
+
+        @pl.loop(1, last)
+        def _(back):
+            for m in range(chs):
+                greet(last - back, m)
+
+        @pl.loop(ch + 1, chs)
+        def _(other):
+            greet(0, other)
+
+    for mate in mates:
+
+        @pl.when((mate > ch) & (row < last) & (here >= cores))
+        def _():
+            greet(row, mate)
+
+    lower_mates = lax.rem(ch, cores) + ch // cores
+    greeted_above = jnp.minimum(ch, cores) + jnp.where(ch < cores, 0, lower_mates - 1)
+    greetings = jnp.where(
+        row == 0,
+        greeted_above,
+        jnp.where(row < last, cores + lower_mates, jnp.where(is_last, rows * chs - 1, cores)),
+    )
+
+    pltpu.make_async_copy(pair_hbm, own_buf, own_sem).start()
+    pltpu.make_async_copy(pair_hbm, block_buf.at[here], block_recv).start()
+    vectors = [
+        (ref, vector_buf.at[ch, t], vector_send, 2)
+        for t, ref in enumerate((bias_hbm, gain_hbm, offset_hbm))
+    ]
+    pieces = (
+        (0, proj_hbm, first_buf, 0, depth),
+        (0, gate_hbm, first_buf, depth, block),
+        (0, mix_hbm, first_buf, depth + block, block),
+        (1, proj_hbm, second_buf, 0, depth),
+        (1, mix_hbm, second_buf, depth, block),
+    )
+    weights = [
+        (ref.at[u], buf.at[ch, pl.ds(at, size)], weight_send.at[u], u)
+        for u, ref, buf, at, size in pieces
+    ]
+    parcels = weights[:3] + vectors + weights[3:]
+    for src, dst, _, k in parcels:
+        pltpu.make_async_copy(src, dst, parcel_recv.at[k]).start()
     pltpu.make_async_copy(mask_hbm, mask_ref, scalar_sem.at[0]).start()
     pltpu.make_async_copy(chain_hbm, chain_ref, scalar_sem.at[1]).start()
-    pltpu.make_async_copy(in_gain_hbm, norm_buf.at[0], norm_sem.at[0]).start()
-    pltpu.make_async_copy(in_bias_hbm, norm_buf.at[1], norm_sem.at[1]).start()
-    here = row * chs + ch
-    pltpu.make_async_copy(pair_hbm, block_buf.at[here], block_recv).start()
-    vectors = [
-        (ref, vector_buf.at[t, ch], vector_send.at[t], vector_recv.at[t])
-        for t, ref in enumerate((bias_hbm, gain_hbm, offset_hbm))
-    ]
-    weights = [
-        [
-            (ref.at[u], buf.at[u, ch], weight_send.at[u, t], weight_recv.at[u, t])
-            for t, (ref, buf) in enumerate(
-                ((proj_hbm, proj_buf), (gate_hbm, gate_buf), (mix_hbm, mix_buf))
-            )
-        ]
-        for u in range(2)
-    ]
-    for src, dst, _, recv in weights[0] + vectors + weights[1]:
-        pltpu.make_async_copy(src, dst, recv).start()
+    pltpu.make_async_copy(in_gain_hbm, norm_buf.at[0], norm_sem).start()
+    pltpu.make_async_copy(in_bias_hbm, norm_buf.at[1], norm_sem).start()
+    pltpu.make_async_copy(gate_hbm.at[1], last_gate_buf, gate_sem).start()
 
     def send(src, dst, send_sem, recv_sem, r, c):
         pltpu.make_async_remote_copy(
@@ -115,30 +159,95 @@
             device_id_type=MESH,
         ).start()
 
-    def send_block(r, c):
-        send(pair_hbm, block_buf.at[here], block_send, block_recv, r, c)
-
-    pl.semaphore_wait(barrier, chs - 1 + row * chs)
-
-    @pl.loop(0, row)
+    def send_block(src, r, c):
+        send(src, block_buf.at[here], block_send, block_recv, r, c)
+
+    def give(step):
+        for src, dst, send_sem, k in parcels:
+            recv_sem = far_recv.at[step, k] if step < len(far) else parcel_recv.at[k]
+            send(src, dst, send_sem, recv_sem, row, mates[step])
+
+    @pl.when(here > 0)
+    def _():
+        pl.semaphore_wait(barrier, greetings)
+
+    for m in range(cores):
+
+        @pl.when(here > m)
+        def _():
+            send_block(pair_hbm, 0, m)
+
+    @pl.when(is_last)
+    def _():
+        @pl.loop(0, last)
+        def _(other):
+            for m in range(chs):
+                pl.semaphore_signal(ready_sem, inc=1, device_id=(other, m), device_id_type=MESH)
+
+        for m in range(chs - 1):
+            pl.semaphore_signal(ready_sem, inc=1, device_id=(last, m), device_id_type=MESH)
+
+    for mate in mates:
+
+        @pl.when((mate < ch) & (row < last))
+        def _():
+            pl.semaphore_signal(near_sem, inc=1, device_id=(row, mate), device_id_type=MESH)
+
+    for step, mate in enumerate(mates):
+
+        @pl.when((mate < ch) & (row < last))
+        def _():
+            give(step)
+
+    @pl.when((row < last) & (ch < chs - 1))
+    def _():
+        pl.semaphore_wait(near_sem, len(mates) - lower_mates)
+
+    @pl.when((row == last) & jnp.logical_not(is_last))
+    def _():
+        pl.semaphore_wait(ready_sem, 1)
+
+    for step, mate in enumerate(mates):
+
+        @pl.when((mate > ch) | (row == last))
+        def _():
+            give(step)
+
+    drain(own_buf, own_sem)
+
+    @pl.when(row < last)
+    def _():
+        pl.semaphore_wait(ready_sem, 1)
+
+    @pl.loop(0, last - row)
+    def _(back):
+        for m in range(chs):
+            send_block(own_buf, last - back, m)
+
+    @pl.loop(1, row)
     def _(other):
         for m in range(chs):
-            send_block(other, m)
-            pl.semaphore_signal(
-                ready_sem.at[row], inc=1, device_id=(other, m), device_id_type=MESH
-            )
-
-    for peer in peers:
-        send_block(row, peer)
-    for src, dst, send_sem, recv_sem in weights[0] + vectors + weights[1]:
-        for peer in peers:
-            send(src, dst, send_sem, recv_sem, row, peer)
-
-    @pl.loop(row + 1, rows)
-    def _(other):
-        pl.semaphore_wait(ready_sem.at[other], chs)
-        for m in range(chs):
-            send_block(other, m)
+            send_block(own_buf, other, m)
+
+    for m in range(1, chs):
+
+        @pl.when(here < m if m < cores else (here != m))
+        def _():
+            send_block(own_buf, 0, m)
+
+    @pl.when(row > 0)
+    def _():
+        for step in range(1, chs):
+            send_block(own_buf, row, lax.rem(ch + step, chs))
+
+    parcel_bufs = (first_buf, second_buf, vector_buf)
+    parcel_sends = (weight_send.at[0], weight_send.at[1], vector_send)
+    for k in (0, 2, 1):
+        for step in range(len(far)):
+            source = lax.rem(ch + chs - cores * (step + 1), chs)
+            piece = parcel_bufs[k].at[source]
+            drain(piece, far_recv.at[step, k])
+            send(piece, piece, parcel_sends[k], parcel_recv.at[k], row, partner)
 
     drain(mask_hbm, scalar_sem.at[0])
     drain(chain_hbm, scalar_sem.at[1])
@@ -154,37 +263,37 @@
     )
     same_here = jnp.where(chain_j == chain_ref[row], 1.0, 0.0).astype(F32)
 
-    def projection(u, part):
-        part_rows = slice(part * block, (part + 1) * block)
-        return proj_buf[u, :, part_rows, :].reshape(lanes, lanes)
-
     def vector(t, u):
-        return jnp.concatenate([vector_buf[t, m, u : u + 1, :] for m in range(chs)], axis=1)
-
-    def arms(u, normed):
-        left = jax.nn.sigmoid(dot_nt(normed, projection(u, 0))) * dot_nt(normed, projection(u, 1))
-        right = jax.nn.sigmoid(dot_nt(normed, projection(u, 2))) * dot_nt(normed, projection(u, 3))
+        return jnp.concatenate([vector_buf[m, t, u : u + 1, :] for m in range(chs)], axis=1)
+
+    drain(norm_buf, norm_sem)
+    drain(vector_buf.at[pl.ds(0, chs - len(far))], parcel_recv.at[2])
+    bias = vector(0, 0) * same_chain
+    gains = [vector(1, u) for u in range(2)]
+    offsets = [vector(2, u) for u in range(2)]
+    last_bias = vector_buf[ch, 0, 1:2, :] * same_here[:, 0:block]
+
+    picked = lax.broadcasted_iota(jnp.int32, (block, lanes), 1)
+    wanted = lax.broadcasted_iota(jnp.int32, (block, lanes), 0) + ch * block
+    chosen = jnp.where(picked == wanted, 1.0, 0.0).astype(BF16)
+    drain(last_gate_buf, gate_sem)
+    drain(first_buf.at[pl.ds(0, chs - len(far))], parcel_recv.at[0])
+    drain(second_buf.at[pl.ds(0, chs - len(far))], parcel_recv.at[1])
+    last_mix = dot_nt(second_buf[:, depth:, :].reshape(lanes, lanes), chosen).astype(BF16)
+
+    def arms(buf, normed):
+        def value(part):
+            part_rows = slice(part * block, (part + 1) * block)
+            return dot_nt(normed, buf[:, part_rows, :].reshape(lanes, lanes))
+
+        left = jax.nn.sigmoid(value(0)) * value(1)
+        right = jax.nn.sigmoid(value(2)) * value(3)
         left_buf[...] = (left * pair_mask).astype(BF16).astype(F32)
         right_buf[...] = (right * pair_mask).astype(BF16).astype(F32)
 
-    def update(u, pair, normed, product, same):
-        xn = lane_norm(product, vector(1, u), vector(2, u))
-        mixed = dot_nn(xn, mix_buf[u].reshape(lanes, lanes))
-        logits = dot_nt(normed, gate_buf[u].reshape(lanes, lanes)) + vector(0, u) * same
-        return (pair + jax.nn.sigmoid(logits) * mixed).astype(BF16)
-
     def normalize(u, pair):
         return lane_norm(pair, norm_buf[0, u : u + 1, :], norm_buf[1, u : u + 1, :])
 
-    def arrive(u):
-        for t, buf in enumerate((proj_buf, gate_buf, mix_buf)):
-            drain(buf.at[u], weight_recv.at[u, t])
-
-    drain(norm_buf.at[0], norm_sem.at[0])
-    drain(norm_buf.at[1], norm_sem.at[1])
-    for t in range(3):
-        drain(vector_buf.at[t], vector_recv.at[t])
-    arrive(0)
     drain(block_buf, block_recv)
     pair = jnp.concatenate(
         [
@@ -194,7 +303,9 @@
         axis=0,
     )
     normed = normalize(0, pair)
-    arms(0, normed)
+    logits = dot_nt(normed, first_buf[:, depth : depth + block, :].reshape(lanes, lanes)) + bias
+    gating = jax.nn.sigmoid(logits)
+    arms(first_buf, normed)
     right_k = [right_buf[pl.ds(k, n, stride=n), :] for k in range(n)]
     product = []
     for i in range(n):
@@ -202,30 +313,28 @@
         for k in range(1, n):
             total = total + left_buf[i * n + k : i * n + k + 1, :] * right_k[k]
         product.append(total)
-    middle = update(0, pair, normed, jnp.concatenate(product, axis=0), same_chain).astype(F32)
+    xn = lane_norm(jnp.concatenate(product, axis=0), gains[0], offsets[0])
+    mixed = dot_nn(xn, first_buf[:, depth + block :, :].reshape(lanes, lanes))
+    middle = (pair + gating * mixed).astype(BF16).astype(F32)
     middle_buf[...] = middle
 
     normed = normalize(1, middle)
     normed_buf[...] = normed.astype(F32)
-    arrive(1)
-    arms(1, normed)
+    mine = pl.ds(pl.multiple_of(row * n, n), n)
+    logits = dot_nt(normed_buf[mine, :].astype(BF16), last_gate_buf[...]) + last_bias
+    gating = jax.nn.sigmoid(logits)
+    kept = dot_nt(middle_buf[mine, :].astype(BF16), chosen)
+    arms(second_buf, normed)
     total = left_buf[pl.ds(row, 1), :] * right_buf[0:n, :]
     for k in range(1, n):
         total = total + left_buf[pl.ds(k * n + row, 1), :] * right_buf[k * n : (k + 1) * n, :]
-    mine = pl.ds(pl.multiple_of(row * n, n), n)
-    result = update(1, middle_buf[mine, :], normed_buf[mine, :].astype(BF16), total, same_here)
-
-    picked = lax.broadcasted_iota(jnp.int32, (block, lanes), 1)
-    wanted = lax.broadcasted_iota(jnp.int32, (block, lanes), 0) + ch * block
-    chosen = jnp.where(picked == wanted, 1.0, 0.0).astype(BF16)
-    out_ref[...] = dot_nt(result, chosen).astype(BF16)
+    xn = lane_norm(total, gains[1], offsets[1])
+    out_ref[...] = (kept + gating * dot_nn(xn, last_mix)).astype(BF16)
 
     drain(block_buf.at[pl.ds(0, rows * chs - 1)], block_send)
-    for t in range(3):
-        drain(vector_buf.at[t, pl.ds(0, chs - 1)], vector_send.at[t])
-    for u in range(2):
-        for t, buf in enumerate((proj_buf, gate_buf, mix_buf)):
-            drain(buf.at[u, pl.ds(0, chs - 1)], weight_send.at[u, t])
+    drain(vector_buf.at[pl.ds(0, chs - 1)], vector_send)
+    drain(first_buf.at[pl.ds(0, chs - 1)], weight_send.at[0])
+    drain(second_buf.at[pl.ds(0, chs - 1)], weight_send.at[1])
 
 
 def window_body(
@@ -258,24 +367,28 @@
             pltpu.SMEM(residue_mask.shape, jnp.int32),
             pltpu.SMEM(chain_ids.shape, jnp.int32),
             pltpu.VMEM((2, layers, lanes), F32),
+            pltpu.VMEM((n, block), BF16),
             pltpu.VMEM((rows * chs, n, block), BF16),
-            pltpu.VMEM((layers, chs, parts * block, lanes), BF16),
-            pltpu.VMEM((layers, chs, block, lanes), BF16),
-            pltpu.VMEM((layers, chs, block, lanes), BF16),
-            pltpu.VMEM((3, chs, layers, block), F32),
+            pltpu.VMEM((chs, (parts + 2) * block, lanes), BF16),
+            pltpu.VMEM((chs, (parts + 1) * block, lanes), BF16),
+            pltpu.VMEM((block, lanes), BF16),
+            pltpu.VMEM((chs, 3, layers, block), F32),
             pltpu.VMEM((n * n, lanes), F32),
             pltpu.VMEM((n * n, lanes), F32),
             pltpu.VMEM((n * n, lanes), F32),
             pltpu.VMEM((n * n, lanes), F32),
-            pltpu.SemaphoreType.REGULAR((rows,)),
-            dma((2,)),
+            pltpu.SemaphoreType.REGULAR,
+            pltpu.SemaphoreType.REGULAR,
             dma((2,)),
             dma,
             dma,
+            dma,
+            dma,
+            dma,
+            dma((2,)),
             dma((3,)),
-            dma((3,)),
-            dma((layers, 3)),
-            dma((layers, 3)),
+            dma((chs // 2 - 1, 3)),
+            dma,
         ],
         compiler_params=pltpu.CompilerParams(collective_id=0, has_side_effects=True),
     )(
@@ -393,7 +506,7 @@
     pair_rep, in_gain = args[0], args[3]
     n, lanes = pair_rep.shape[2], in_gain.shape[1]
     one_tile = pair_rep.shape[1] == 1 and n == rows == 8 and lanes == 128
-    if one_tile and chs > 1 and args[5].shape[1] == pair_rep.shape[0] * chs:
+    if one_tile and chs > 2 and chs % 2 == 0 and args[5].shape[1] == pair_rep.shape[0] * chs:
         return window_body(rows, chs, *args)
     return body(*args)
 

time: 12.3 us -> 11 us (0.89)
  the two profiles are of different devices: /device:TPU:25 before, /device:TPU:0 now
where the time goes in v2:
time: 11 us; the launch traced here: 10.9 us
  Pallas kernels  10.3 us (94%)
  local copies, waits for them, and re-layouts  0.58 us (5%)
    pallas_call x1, Pallas kernels, window_body(): pl.pallas_call(functools.partial(window_kernel, rows, chs), out_shape=plt...  10.3 us
    unnamed x1, local copies, waits for them, and re-layouts  0.58 us

profile of v2, /device:TPU:0, one launch (start us, length us, event | category | flops | bytes accessed | tf_op | source)
XLA Modules:
  0.0 10.9 jit_solution(8776924638935939155)
XLA Ops:
  0.0 10.3 %shard_map.109 = bf16[8,32]{1,0:T(8,128)(2,1)S(1)} custom-call(s32[8]{0:T(128)} %mask_hbm.1, s32[8]{0:T(128)} %chain_hbm.1, bf16[8,32]{1,0:T(8,128)(2,1)} %bitcast.13, f32[2,128]{1,0:T(2,128)} %in_gain_hbm.1, f32[2,128]{1,0:T(2,128)} %in_bias_hbm.1, bf16[2,128,128]{2,1,0:T(8,128)(2,1)} %bitcast.11, bf16[2,32,128]{2,1,0:T(8,128)(2,1)} %bitcast.12, ...), custom_call_target="tpu_custom_call" | custom-call | tf_op jit(solution)/shard_map/pallas_call | solution.py:361
  10.3 0.6 %copy.13 = bf16[32,1,8]{0,2,1:T(8,128)(2,1)} copy(bf16[32,1,8]{0,2,1:T(8,128)(2,1)S(1)} %bitcast.10) | data formatting | bytes 1024

commit v3 on v2

--- a/solution.py
+++ b/solution.py
@@ -57,7 +57,6 @@
     left_buf,
     right_buf,
     middle_buf,
-    normed_buf,
     near_sem,
     ready_sem,
     scalar_sem,
@@ -213,7 +212,22 @@
         def _():
             give(step)
 
+    def pass_on():
+        for k, buf, send_sem in (
+            (0, first_buf, weight_send.at[0]),
+            (2, vector_buf, vector_send),
+            (1, second_buf, weight_send.at[1]),
+        ):
+            for step in range(len(far)):
+                piece = buf.at[lax.rem(ch + chs - cores * (step + 1), chs)]
+                drain(piece, far_recv.at[step, k])
+                send(piece, piece, send_sem, parcel_recv.at[k], row, partner)
+
     drain(own_buf, own_sem)
+
+    @pl.when(here < cores)
+    def _():
+        pass_on()
 
     @pl.when(row < last)
     def _():
@@ -240,14 +254,9 @@
         for step in range(1, chs):
             send_block(own_buf, row, lax.rem(ch + step, chs))
 
-    parcel_bufs = (first_buf, second_buf, vector_buf)
-    parcel_sends = (weight_send.at[0], weight_send.at[1], vector_send)
-    for k in (0, 2, 1):
-        for step in range(len(far)):
-            source = lax.rem(ch + chs - cores * (step + 1), chs)
-            piece = parcel_bufs[k].at[source]
-            drain(piece, far_recv.at[step, k])
-            send(piece, piece, parcel_sends[k], parcel_recv.at[k], row, partner)
+    @pl.when(here >= cores)
+    def _():
+        pass_on()
 
     drain(mask_hbm, scalar_sem.at[0])
     drain(chain_hbm, scalar_sem.at[1])
@@ -276,23 +285,87 @@
     picked = lax.broadcasted_iota(jnp.int32, (block, lanes), 1)
     wanted = lax.broadcasted_iota(jnp.int32, (block, lanes), 0) + ch * block
     chosen = jnp.where(picked == wanted, 1.0, 0.0).astype(BF16)
+    diagonal = lax.broadcasted_iota(jnp.int32, (lanes, lanes), 0) == lax.broadcasted_iota(
+        jnp.int32, (lanes, lanes), 1
+    )
+    def halves(values):
+        high = values.astype(BF16)
+        return high, (values - high.astype(F32)).astype(BF16)
+
+    def tail_of(*rows_of):
+        count = 2 * n
+        place_of = lax.broadcasted_iota(jnp.int32, (count, rows_of[0].shape[1]), 0)
+        tail = jnp.zeros(place_of.shape, F32)
+        for i, values in enumerate(rows_of):
+            tail = jnp.where(place_of == i, values.astype(F32), tail)
+        return tail.astype(BF16)
+
+    one = jnp.ones((1, lanes), F32)
+    in_tails, out_tails = [], []
+    for u in range(2):
+        ratio = norm_buf[1, u : u + 1, :] / norm_buf[0, u : u + 1, :]
+        in_tails.append(tail_of(one, *halves(ratio)))
+        ratio = offsets[u] / gains[u]
+        out_tails.append(
+            tail_of(
+                jnp.concatenate([one, 0.0 * one], axis=1), jnp.concatenate(halves(ratio), axis=1)
+            )
+        )
+
+    def statistics(values):
+        mean_val = jnp.mean(values, axis=-1, keepdims=True)
+        variance = jnp.mean(values * values, axis=-1, keepdims=True) - mean_val * mean_val
+        scale = lax.rsqrt(variance + epsilon)
+        return scale, scale * mean_val
+
+    def normed_product(product, stats):
+        count = stats[0].shape[0]
+        total = product[count : count + 1]
+        shift = product[count + 1 : count + 2] + product[count + 2 : count + 3]
+        return product[0:count] * stats[0] + (shift - stats[1] * total)
+
+    def fold_in(u, weight):
+        return (weight.astype(F32) * norm_buf[0, u : u + 1, :]).astype(BF16)
+
+    def fold_out(u, weight):
+        column = jnp.sum(jnp.where(diagonal, gains[u], 0.0), axis=-1, keepdims=True)
+        scaled = (weight.astype(F32) * column).astype(BF16)
+        return jnp.concatenate([scaled, scaled], axis=0)
+
+    def parts_of(u, buf):
+        return [
+            fold_in(u, buf[:, part * block : (part + 1) * block, :].reshape(lanes, lanes))
+            for part in range(depth // block)
+        ]
+
+    def with_tail(values, tail):
+        return jnp.concatenate([values, tail], axis=0)
+
+    def arms(lhs, stats, folded):
+        value = [normed_product(dot_nt(lhs, part), stats) for part in folded]
+        left_buf[...] = (
+            (jax.nn.sigmoid(value[0]) * value[1] * pair_mask).astype(BF16).astype(F32)
+        )
+        right_buf[...] = (
+            (jax.nn.sigmoid(value[2]) * value[3] * pair_mask).astype(BF16).astype(F32)
+        )
+
+    def mix(u, values, folded):
+        both = [half.astype(F32) for half in halves(values)]
+        lhs = with_tail(jnp.concatenate(both, axis=1), out_tails[u].astype(F32)).astype(BF16)
+        return normed_product(dot_nn(lhs, folded), statistics(values))
+
     drain(last_gate_buf, gate_sem)
     drain(first_buf.at[pl.ds(0, chs - len(far))], parcel_recv.at[0])
+    first_parts = parts_of(0, first_buf)
+    first_gate = fold_in(0, first_buf[:, depth : depth + block, :].reshape(lanes, lanes))
+    first_mix = fold_out(0, first_buf[:, depth + block :, :].reshape(lanes, lanes))
     drain(second_buf.at[pl.ds(0, chs - len(far))], parcel_recv.at[1])
-    last_mix = dot_nt(second_buf[:, depth:, :].reshape(lanes, lanes), chosen).astype(BF16)
-
-    def arms(buf, normed):
-        def value(part):
-            part_rows = slice(part * block, (part + 1) * block)
-            return dot_nt(normed, buf[:, part_rows, :].reshape(lanes, lanes))
-
-        left = jax.nn.sigmoid(value(0)) * value(1)
-        right = jax.nn.sigmoid(value(2)) * value(3)
-        left_buf[...] = (left * pair_mask).astype(BF16).astype(F32)
-        right_buf[...] = (right * pair_mask).astype(BF16).astype(F32)
-
-    def normalize(u, pair):
-        return lane_norm(pair, norm_buf[0, u : u + 1, :], norm_buf[1, u : u + 1, :])
+    second_parts = parts_of(1, second_buf)
+    last_gate = fold_in(1, last_gate_buf[...])
+    last_mix = fold_out(
+        1, dot_nt(second_buf[:, depth:, :].reshape(lanes, lanes), chosen).astype(BF16)
+    )
 
     drain(block_buf, block_recv)
     pair = jnp.concatenate(
@@ -302,10 +375,11 @@
         ],
         axis=0,
     )
-    normed = normalize(0, pair)
-    logits = dot_nt(normed, first_buf[:, depth : depth + block, :].reshape(lanes, lanes)) + bias
+    lhs = with_tail(pair.astype(BF16), in_tails[0])
+    stats = statistics(pair)
+    arms(lhs, stats, first_parts)
+    logits = normed_product(dot_nt(lhs, first_gate), stats) + bias
     gating = jax.nn.sigmoid(logits)
-    arms(first_buf, normed)
     right_k = [right_buf[pl.ds(k, n, stride=n), :] for k in range(n)]
     product = []
     for i in range(n):
@@ -313,23 +387,21 @@
         for k in range(1, n):
             total = total + left_buf[i * n + k : i * n + k + 1, :] * right_k[k]
         product.append(total)
-    xn = lane_norm(jnp.concatenate(product, axis=0), gains[0], offsets[0])
-    mixed = dot_nn(xn, first_buf[:, depth + block :, :].reshape(lanes, lanes))
-    middle = (pair + gating * mixed).astype(BF16).astype(F32)
+    mixed = mix(0, jnp.concatenate(product, axis=0), first_mix)
+    values = (pair + gating * mixed).astype(BF16)
+    middle = values.astype(F32)
     middle_buf[...] = middle
 
-    normed = normalize(1, middle)
-    normed_buf[...] = normed.astype(F32)
-    mine = pl.ds(pl.multiple_of(row * n, n), n)
-    logits = dot_nt(normed_buf[mine, :].astype(BF16), last_gate_buf[...]) + last_bias
-    gating = jax.nn.sigmoid(logits)
-    kept = dot_nt(middle_buf[mine, :].astype(BF16), chosen)
-    arms(second_buf, normed)
+    arms(with_tail(values, in_tails[1]), statistics(middle), second_parts)
+    mine = middle_buf[pl.ds(pl.multiple_of(row * n, n), n), :]
+    near_lhs = with_tail(mine, in_tails[1].astype(F32)).astype(BF16)
+    logits = normed_product(dot_nt(near_lhs, last_gate), statistics(mine))
+    gating = jax.nn.sigmoid(logits + last_bias)
+    kept = dot_nt(mine.astype(BF16), chosen)
     total = left_buf[pl.ds(row, 1), :] * right_buf[0:n, :]
     for k in range(1, n):
         total = total + left_buf[pl.ds(k * n + row, 1), :] * right_buf[k * n : (k + 1) * n, :]
-    xn = lane_norm(total, gains[1], offsets[1])
-    out_ref[...] = (kept + gating * dot_nn(xn, last_mix)).astype(BF16)
+    out_ref[...] = (kept + gating * mix(1, total, last_mix)).astype(BF16)
 
     drain(block_buf.at[pl.ds(0, rows * chs - 1)], block_send)
     drain(vector_buf.at[pl.ds(0, chs - 1)], vector_send)
@@ -376,7 +448,6 @@
             pltpu.VMEM((n * n, lanes), F32),
             pltpu.VMEM((n * n, lanes), F32),
             pltpu.VMEM((n * n, lanes), F32),
-            pltpu.VMEM((n * n, lanes), F32),
             pltpu.SemaphoreType.REGULAR,
             pltpu.SemaphoreType.REGULAR,
             dma((2,)),

time: 11 us -> 10.7 us (0.973)
  Pallas kernels: 10.3 us -> 9.94 us
    pallas_call x1, Pallas kernels: 10.3 us -> 9.94 us  [window_body(): pl.pallas_call(functools.partial(window_kernel, rows, chs), out_shape=plt...]
where the time goes in v3:
time: 10.7 us; the launch traced here: 10.5 us
  Pallas kernels  9.94 us (93%)
  local copies, waits for them, and re-layouts  0.58 us (5%)
    pallas_call x1, Pallas kernels, window_body(): pl.pallas_call(functools.partial(window_kernel, rows, chs), out_shape=plt...  9.94 us
    unnamed x1, local copies, waits for them, and re-layouts  0.58 us

profile of v3, /device:TPU:0, one launch (start us, length us, event | category | flops | bytes accessed | tf_op | source)
XLA Modules:
  0.0 10.5 jit_solution(4608718635968655858)
XLA Ops:
  0.0 9.9 %shard_map.109 = bf16[8,32]{1,0:T(8,128)(2,1)S(1)} custom-call(s32[8]{0:T(128)} %mask_hbm.1, s32[8]{0:T(128)} %chain_hbm.1, bf16[8,32]{1,0:T(8,128)(2,1)} %bitcast.13, f32[2,128]{1,0:T(2,128)} %in_gain_hbm.1, f32[2,128]{1,0:T(2,128)} %in_bias_hbm.1, bf16[2,128,128]{2,1,0:T(8,128)(2,1)} %bitcast.11, bf16[2,32,128]{2,1,0:T(8,128)(2,1)} %bitcast.12, ...), custom_call_target="tpu_custom_call" | custom-call | tf_op jit(solution)/shard_map/pallas_call | solution.py:433
  10.0 0.6 %copy.13 = bf16[32,1,8]{0,2,1:T(8,128)(2,1)} copy(bf16[32,1,8]{0,2,1:T(8,128)(2,1)S(1)} %bitcast.10) | data formatting | bytes 1024

commit v4 on v3

--- a/solution.py
+++ b/solution.py
@@ -305,12 +305,7 @@
     for u in range(2):
         ratio = norm_buf[1, u : u + 1, :] / norm_buf[0, u : u + 1, :]
         in_tails.append(tail_of(one, *halves(ratio)))
-        ratio = offsets[u] / gains[u]
-        out_tails.append(
-            tail_of(
-                jnp.concatenate([one, 0.0 * one], axis=1), jnp.concatenate(halves(ratio), axis=1)
-            )
-        )
+        out_tails.append(tail_of(one, *halves(offsets[u] / gains[u])))
 
     def statistics(values):
         mean_val = jnp.mean(values, axis=-1, keepdims=True)
@@ -318,19 +313,24 @@
         scale = lax.rsqrt(variance + epsilon)
         return scale, scale * mean_val
 
-    def normed_product(product, stats):
-        count = stats[0].shape[0]
-        total = product[count : count + 1]
-        shift = product[count + 1 : count + 2] + product[count + 2 : count + 3]
-        return product[0:count] * stats[0] + (shift - stats[1] * total)
+    def sigmoid(values):
+        return 0.5 * jnp.tanh(0.5 * values) + 0.5
+
+    def fold(dot, scaled, tail):
+        product = dot(tail, scaled)
+        return scaled, product[0:1], product[1:2] + product[2:3]
+
+    def normed_product(product, stats, folded):
+        return product * stats[0] + (folded[2] - stats[1] * folded[1])
 
     def fold_in(u, weight):
-        return (weight.astype(F32) * norm_buf[0, u : u + 1, :]).astype(BF16)
+        scaled = (weight.astype(F32) * norm_buf[0, u : u + 1, :]).astype(BF16)
+        return fold(dot_nt, scaled, in_tails[u])
 
     def fold_out(u, weight):
         column = jnp.sum(jnp.where(diagonal, gains[u], 0.0), axis=-1, keepdims=True)
         scaled = (weight.astype(F32) * column).astype(BF16)
-        return jnp.concatenate([scaled, scaled], axis=0)
+        return fold(dot_nn, scaled, out_tails[u])
 
     def parts_of(u, buf):
         return [
@@ -338,22 +338,15 @@
             for part in range(depth // block)
         ]
 
-    def with_tail(values, tail):
-        return jnp.concatenate([values, tail], axis=0)
-
-    def arms(lhs, stats, folded):
-        value = [normed_product(dot_nt(lhs, part), stats) for part in folded]
-        left_buf[...] = (
-            (jax.nn.sigmoid(value[0]) * value[1] * pair_mask).astype(BF16).astype(F32)
-        )
-        right_buf[...] = (
-            (jax.nn.sigmoid(value[2]) * value[3] * pair_mask).astype(BF16).astype(F32)
-        )
-
-    def mix(u, values, folded):
-        both = [half.astype(F32) for half in halves(values)]
-        lhs = with_tail(jnp.concatenate(both, axis=1), out_tails[u].astype(F32)).astype(BF16)
-        return normed_product(dot_nn(lhs, folded), statistics(values))
+    def arms(values, stats, folded):
+        value = [normed_product(dot_nt(values, part[0]), stats, part) for part in folded]
+        left_buf[...] = sigmoid(value[0]) * (value[1] * pair_mask)
+        right_buf[...] = sigmoid(value[2]) * (value[3] * pair_mask)
+
+    def mix(values, folded):
+        both = jnp.concatenate(halves(values), axis=1)
+        product = dot_nn(both, jnp.concatenate([folded[0], folded[0]], axis=0))
+        return normed_product(product, statistics(values), folded)
 
     drain(last_gate_buf, gate_sem)
     drain(first_buf.at[pl.ds(0, chs - len(far))], parcel_recv.at[0])
@@ -375,11 +368,10 @@
         ],
         axis=0,
     )
-    lhs = with_tail(pair.astype(BF16), in_tails[0])
+    values = pair.astype(BF16)
     stats = statistics(pair)
-    arms(lhs, stats, first_parts)
-    logits = normed_product(dot_nt(lhs, first_gate), stats) + bias
-    gating = jax.nn.sigmoid(logits)
+    arms(values, stats, first_parts)
+    gating = sigmoid(normed_product(dot_nt(values, first_gate[0]), stats, first_gate) + bias)
     right_k = [right_buf[pl.ds(k, n, stride=n), :] for k in range(n)]
     product = []
     for i in range(n):
@@ -387,21 +379,20 @@
         for k in range(1, n):
             total = total + left_buf[i * n + k : i * n + k + 1, :] * right_k[k]
         product.append(total)
-    mixed = mix(0, jnp.concatenate(product, axis=0), first_mix)
+    mixed = mix(jnp.concatenate(product, axis=0), first_mix)
     values = (pair + gating * mixed).astype(BF16)
     middle = values.astype(F32)
     middle_buf[...] = middle
 
-    arms(with_tail(values, in_tails[1]), statistics(middle), second_parts)
+    arms(values, statistics(middle), second_parts)
     mine = middle_buf[pl.ds(pl.multiple_of(row * n, n), n), :]
-    near_lhs = with_tail(mine, in_tails[1].astype(F32)).astype(BF16)
-    logits = normed_product(dot_nt(near_lhs, last_gate), statistics(mine))
-    gating = jax.nn.sigmoid(logits + last_bias)
+    logits = normed_product(dot_nt(mine.astype(BF16), last_gate[0]), statistics(mine), last_gate)
+    gating = sigmoid(logits + last_bias)
     kept = dot_nt(mine.astype(BF16), chosen)
     total = left_buf[pl.ds(row, 1), :] * right_buf[0:n, :]
     for k in range(1, n):
         total = total + left_buf[pl.ds(k * n + row, 1), :] * right_buf[k * n : (k + 1) * n, :]
-    out_ref[...] = (kept + gating * mix(1, total, last_mix)).astype(BF16)
+    out_ref[...] = (kept + gating * mix(total, last_mix)).astype(BF16)
 
     drain(block_buf.at[pl.ds(0, rows * chs - 1)], block_send)
     drain(vector_buf.at[pl.ds(0, chs - 1)], vector_send)

time: 10.7 us -> 10.6 us (level)
  no operation moved by 1% of the time
where the time goes in v4:
time: 10.6 us; the launch traced here: 10.5 us
  Pallas kernels  9.87 us (93%)
  local copies, waits for them, and re-layouts  0.58 us (5%)
    pallas_call x1, Pallas kernels, window_body(): pl.pallas_call(functools.partial(window_kernel, rows, chs), out_shape=plt...  9.87 us
    unnamed x1, local copies, waits for them, and re-layouts  0.58 us

profile of v4, /device:TPU:0, one launch (start us, length us, event | category | flops | bytes accessed | tf_op | source)
XLA Modules:
  0.0 10.5 jit_solution(7317285158143102627)
XLA Ops:
  0.0 9.9 %shard_map.109 = bf16[8,32]{1,0:T(8,128)(2,1)S(1)} custom-call(s32[8]{0:T(128)} %mask_hbm.1, s32[8]{0:T(128)} %chain_hbm.1, bf16[8,32]{1,0:T(8,128)(2,1)} %bitcast.13, f32[2,128]{1,0:T(2,128)} %in_gain_hbm.1, f32[2,128]{1,0:T(2,128)} %in_bias_hbm.1, bf16[2,128,128]{2,1,0:T(8,128)(2,1)} %bitcast.11, bf16[2,32,128]{2,1,0:T(8,128)(2,1)} %bitcast.12, ...), custom_call_target="tpu_custom_call" | custom-call | tf_op jit(solution)/shard_map/pallas_call | solution.py:424
  9.9 0.6 %copy.13 = bf16[32,1,8]{0,2,1:T(8,128)(2,1)} copy(bf16[32,1,8]{0,2,1:T(8,128)(2,1)S(1)} %bitcast.10) | data formatting | bytes 1024

commit v5 on v4

--- a/solution.py
+++ b/solution.py
@@ -122,8 +122,47 @@
         jnp.where(row < last, cores + lower_mates, jnp.where(is_last, rows * chs - 1, cores)),
     )
 
+    def send(src, dst, send_sem, recv_sem, r, c):
+        pltpu.make_async_remote_copy(
+            src_ref=src,
+            dst_ref=dst,
+            send_sem=send_sem,
+            recv_sem=recv_sem,
+            device_id=(r, c),
+            device_id_type=MESH,
+        ).start()
+
+    def send_block(src, r, c):
+        send(src, block_buf.at[ch * rows + row], block_send, block_recv, r, c)
+
+    @pl.when(here > 0)
+    def _():
+        pl.semaphore_wait(barrier, greetings)
+
+    for m in range(cores):
+
+        @pl.when(here > m)
+        def _():
+            send_block(pair_hbm, 0, m)
+
+    @pl.when(is_last)
+    def _():
+        @pl.loop(0, last)
+        def _(other):
+            for m in range(chs):
+                pl.semaphore_signal(ready_sem, inc=1, device_id=(other, m), device_id_type=MESH)
+
+        for m in range(chs - 1):
+            pl.semaphore_signal(ready_sem, inc=1, device_id=(last, m), device_id_type=MESH)
+
+    for mate in mates:
+
+        @pl.when((mate < ch) & (row < last))
+        def _():
+            pl.semaphore_signal(near_sem, inc=1, device_id=(row, mate), device_id_type=MESH)
+
     pltpu.make_async_copy(pair_hbm, own_buf, own_sem).start()
-    pltpu.make_async_copy(pair_hbm, block_buf.at[here], block_recv).start()
+    pltpu.make_async_copy(pair_hbm, block_buf.at[ch * rows + row], block_recv).start()
     vectors = [
         (ref, vector_buf.at[ch, t], vector_send, 2)
         for t, ref in enumerate((bias_hbm, gain_hbm, offset_hbm))
@@ -148,49 +187,10 @@
     pltpu.make_async_copy(in_bias_hbm, norm_buf.at[1], norm_sem).start()
     pltpu.make_async_copy(gate_hbm.at[1], last_gate_buf, gate_sem).start()
 
-    def send(src, dst, send_sem, recv_sem, r, c):
-        pltpu.make_async_remote_copy(
-            src_ref=src,
-            dst_ref=dst,
-            send_sem=send_sem,
-            recv_sem=recv_sem,
-            device_id=(r, c),
-            device_id_type=MESH,
-        ).start()
-
-    def send_block(src, r, c):
-        send(src, block_buf.at[here], block_send, block_recv, r, c)
-
     def give(step):
         for src, dst, send_sem, k in parcels:
             recv_sem = far_recv.at[step, k] if step < len(far) else parcel_recv.at[k]
             send(src, dst, send_sem, recv_sem, row, mates[step])
-
-    @pl.when(here > 0)
-    def _():
-        pl.semaphore_wait(barrier, greetings)
-
-    for m in range(cores):
-
-        @pl.when(here > m)
-        def _():
-            send_block(pair_hbm, 0, m)
-
-    @pl.when(is_last)
-    def _():
-        @pl.loop(0, last)
-        def _(other):
-            for m in range(chs):
-                pl.semaphore_signal(ready_sem, inc=1, device_id=(other, m), device_id_type=MESH)
-
-        for m in range(chs - 1):
-            pl.semaphore_signal(ready_sem, inc=1, device_id=(last, m), device_id_type=MESH)
-
-    for mate in mates:
-
-        @pl.when((mate < ch) & (row < last))
-        def _():
-            pl.semaphore_signal(near_sem, inc=1, device_id=(row, mate), device_id_type=MESH)
 
     for step, mate in enumerate(mates):
 
@@ -233,17 +233,7 @@
     def _():
         pl.semaphore_wait(ready_sem, 1)
 
-    @pl.loop(0, last - row)
-    def _(back):
-        for m in range(chs):
-            send_block(own_buf, last - back, m)
-
-    @pl.loop(1, row)
-    def _(other):
-        for m in range(chs):
-            send_block(own_buf, other, m)
-
-    for m in range(1, chs):
+    for m in reversed(range(1, chs)):
 
         @pl.when(here < m if m < cores else (here != m))
         def _():
@@ -253,6 +243,16 @@
     def _():
         for step in range(1, chs):
             send_block(own_buf, row, lax.rem(ch + step, chs))
+
+    @pl.loop(1, row)
+    def _(other):
+        for m in reversed(range(chs)):
+            send_block(own_buf, other, m)
+
+    @pl.loop(row + 1, rows)
+    def _(other):
+        for m in reversed(range(chs)):
+            send_block(own_buf, other, m)
 
     @pl.when(here >= cores)
     def _():
@@ -333,13 +333,22 @@
         return fold(dot_nn, scaled, out_tails[u])
 
     def parts_of(u, buf):
-        return [
-            fold_in(u, buf[:, part * block : (part + 1) * block, :].reshape(lanes, lanes))
+        weights = [
+            buf[:, part * block : (part + 1) * block, :].reshape(lanes, lanes)
             for part in range(depth // block)
         ]
+        return [
+            fold_in(u, jnp.concatenate(weights[first : first + 4], axis=0))
+            for first in range(0, len(weights), 4)
+        ]
 
     def arms(values, stats, folded):
         value = [normed_product(dot_nt(values, part[0]), stats, part) for part in folded]
+        value = [
+            wide[:, first : first + lanes]
+            for wide in value
+            for first in range(0, wide.shape[1], lanes)
+        ]
         left_buf[...] = sigmoid(value[0]) * (value[1] * pair_mask)
         right_buf[...] = sigmoid(value[2]) * (value[3] * pair_mask)
 
@@ -361,14 +370,10 @@
     )
 
     drain(block_buf, block_recv)
-    pair = jnp.concatenate(
-        [
-            jnp.concatenate([block_buf[i * chs + m].astype(F32) for m in range(chs)], axis=1)
-            for i in range(n)
-        ],
-        axis=0,
-    )
-    values = pair.astype(BF16)
+    values = jnp.concatenate(
+        [block_buf[m * rows : (m + 1) * rows].reshape(n * n, block) for m in range(chs)], axis=1
+    )
+    pair = values.astype(F32)
     stats = statistics(pair)
     arms(values, stats, first_parts)
     gating = sigmoid(normed_product(dot_nt(values, first_gate[0]), stats, first_gate) + bias)

time: 10.6 us -> 10.3 us (0.972)
  Pallas kernels: 9.87 us -> 9.58 us
    pallas_call x1, Pallas kernels: 9.87 us -> 9.58 us  [window_body(): pl.pallas_call(functools.partial(window_kernel, rows, chs), out_shape=plt...]
where the time goes in v5:
time: 10.3 us; the launch traced here: 10.2 us
  Pallas kernels  9.58 us (93%)
  local copies, waits for them, and re-layouts  0.58 us (6%)
    pallas_call x1, Pallas kernels, window_body(): pl.pallas_call(functools.partial(window_kernel, rows, chs), out_shape=plt...  9.58 us
    unnamed x1, local copies, waits for them, and re-layouts  0.58 us

profile of v5, /device:TPU:0, one launch (start us, length us, event | category | flops | bytes accessed | tf_op | source)
XLA Modules:
  0.0 10.2 jit_solution(13084842573025578831)
XLA Ops:
  0.0 9.6 %shard_map.109 = bf16[8,32]{1,0:T(8,128)(2,1)S(1)} custom-call(s32[8]{0:T(128)} %mask_hbm.1, s32[8]{0:T(128)} %chain_hbm.1, bf16[8,32]{1,0:T(8,128)(2,1)} %bitcast.13, f32[2,128]{1,0:T(2,128)} %in_gain_hbm.1, f32[2,128]{1,0:T(2,128)} %in_bias_hbm.1, bf16[2,128,128]{2,1,0:T(8,128)(2,1)} %bitcast.11, bf16[2,32,128]{2,1,0:T(8,128)(2,1)} %bitcast.12, ...), custom_call_target="tpu_custom_call" | custom-call | tf_op jit(solution)/shard_map/pallas_call | solution.py:429
  9.6 0.6 %copy.13 = bf16[32,1,8]{0,2,1:T(8,128)(2,1)} copy(bf16[32,1,8]{0,2,1:T(8,128)(2,1)S(1)} %bitcast.10) | data formatting | bytes 1024

commit v6 on v5

--- a/solution.py
+++ b/solution.py
@@ -277,10 +277,10 @@
 
     drain(norm_buf, norm_sem)
     drain(vector_buf.at[pl.ds(0, chs - len(far))], parcel_recv.at[2])
-    bias = vector(0, 0) * same_chain
+    bias = (0.5 * vector(0, 0)) * same_chain
     gains = [vector(1, u) for u in range(2)]
     offsets = [vector(2, u) for u in range(2)]
-    last_bias = vector_buf[ch, 0, 1:2, :] * same_here[:, 0:block]
+    last_bias = (0.5 * vector_buf[ch, 0, 1:2, :]) * same_here[:, 0:block]
 
     picked = lax.broadcasted_iota(jnp.int32, (block, lanes), 1)
     wanted = lax.broadcasted_iota(jnp.int32, (block, lanes), 0) + ch * block
@@ -313,8 +313,8 @@
         scale = lax.rsqrt(variance + epsilon)
         return scale, scale * mean_val
 
-    def sigmoid(values):
-        return 0.5 * jnp.tanh(0.5 * values) + 0.5
+    def gate_of(values):
+        return jnp.tanh(values) + 1.0
 
     def fold(dot, scaled, tail):
         product = dot(tail, scaled)
@@ -324,12 +324,12 @@
         return product * stats[0] + (folded[2] - stats[1] * folded[1])
 
     def fold_in(u, weight):
-        scaled = (weight.astype(F32) * norm_buf[0, u : u + 1, :]).astype(BF16)
+        scaled = (weight.astype(F32) * (0.5 * norm_buf[0, u : u + 1, :])).astype(BF16)
         return fold(dot_nt, scaled, in_tails[u])
 
     def fold_out(u, weight):
         column = jnp.sum(jnp.where(diagonal, gains[u], 0.0), axis=-1, keepdims=True)
-        scaled = (weight.astype(F32) * column).astype(BF16)
+        scaled = (weight.astype(F32) * (0.5 * column)).astype(BF16)
         return fold(dot_nn, scaled, out_tails[u])
 
     def parts_of(u, buf):
@@ -349,8 +349,8 @@
             for wide in value
             for first in range(0, wide.shape[1], lanes)
         ]
-        left_buf[...] = sigmoid(value[0]) * (value[1] * pair_mask)
-        right_buf[...] = sigmoid(value[2]) * (value[3] * pair_mask)
+        left_buf[...] = gate_of(value[0]) * (value[1] * pair_mask)
+        right_buf[...] = gate_of(value[2]) * (value[3] * pair_mask)
 
     def mix(values, folded):
         both = jnp.concatenate(halves(values), axis=1)
@@ -376,7 +376,7 @@
     pair = values.astype(F32)
     stats = statistics(pair)
     arms(values, stats, first_parts)
-    gating = sigmoid(normed_product(dot_nt(values, first_gate[0]), stats, first_gate) + bias)
+    gating = gate_of(normed_product(dot_nt(values, first_gate[0]), stats, first_gate) + bias)
     right_k = [right_buf[pl.ds(k, n, stride=n), :] for k in range(n)]
     product = []
     for i in range(n):
@@ -392,7 +392,7 @@
     arms(values, statistics(middle), second_parts)
     mine = middle_buf[pl.ds(pl.multiple_of(row * n, n), n), :]
     logits = normed_product(dot_nt(mine.astype(BF16), last_gate[0]), statistics(mine), last_gate)
-    gating = sigmoid(logits + last_bias)
+    gating = gate_of(logits + last_bias)
     kept = dot_nt(mine.astype(BF16), chosen)
     total = left_buf[pl.ds(row, 1), :] * right_buf[0:n, :]
     for k in range(1, n):

time: 10.3 us -> 10.3 us (level)
  no operation moved by 1% of the time
where the time goes in v6:
time: 10.3 us; the launch traced here: 10.2 us
  Pallas kernels  9.57 us (93%)
  local copies, waits for them, and re-layouts  0.58 us (6%)
    pallas_call x1, Pallas kernels, window_body(): pl.pallas_call(functools.partial(window_kernel, rows, chs), out_shape=plt...  9.57 us
    unnamed x1, local copies, waits for them, and re-layouts  0.58 us

profile of v6, /device:TPU:0, one launch (start us, length us, event | category | flops | bytes accessed | tf_op | source)
XLA Modules:
  0.0 10.2 jit_solution(6159374085478321155)
XLA Ops:
  0.0 9.6 %shard_map.109 = bf16[8,32]{1,0:T(8,128)(2,1)S(1)} custom-call(s32[8]{0:T(128)} %mask_hbm.1, s32[8]{0:T(128)} %chain_hbm.1, bf16[8,32]{1,0:T(8,128)(2,1)} %bitcast.13, f32[2,128]{1,0:T(2,128)} %in_gain_hbm.1, f32[2,128]{1,0:T(2,128)} %in_bias_hbm.1, bf16[2,128,128]{2,1,0:T(8,128)(2,1)} %bitcast.11, bf16[2,32,128]{2,1,0:T(8,128)(2,1)} %bitcast.12, ...), custom_call_target="tpu_custom_call" | custom-call | tf_op jit(solution)/shard_map/pallas_call | solution.py:429
  9.6 0.6 %copy.13 = bf16[32,1,8]{0,2,1:T(8,128)(2,1)} copy(bf16[32,1,8]{0,2,1:T(8,128)(2,1)S(1)} %bitcast.10) | data formatting | bytes 1024

commit v7 on v6

--- a/solution.py
+++ b/solution.py
@@ -50,8 +50,7 @@
     norm_buf,
     own_buf,
     block_buf,
-    first_buf,
-    second_buf,
+    weight_buf,
     last_gate_buf,
     vector_buf,
     left_buf,
@@ -74,6 +73,7 @@
     lanes = norm_buf.shape[2]
     block = lanes // chs
     depth = proj_hbm.shape[1]
+    split = depth + 2 * block
     row = lax.axis_index("row")
     ch = lax.axis_index("ch")
     here = row * chs + ch
@@ -168,14 +168,14 @@
         for t, ref in enumerate((bias_hbm, gain_hbm, offset_hbm))
     ]
     pieces = (
-        (0, proj_hbm, first_buf, 0, depth),
-        (0, gate_hbm, first_buf, depth, block),
-        (0, mix_hbm, first_buf, depth + block, block),
-        (1, proj_hbm, second_buf, 0, depth),
-        (1, mix_hbm, second_buf, depth, block),
+        (0, proj_hbm, weight_buf, 0, depth),
+        (0, gate_hbm, weight_buf, depth, block),
+        (0, mix_hbm, weight_buf, depth + block, block),
+        (1, proj_hbm, weight_buf, split, depth),
+        (1, mix_hbm, weight_buf, split + depth, block),
     )
     weights = [
-        (ref.at[u], buf.at[ch, pl.ds(at, size)], weight_send.at[u], u)
+        (ref.at[u], buf.at[ch, pl.ds(at, size)], weight_send, u)
         for u, ref, buf, at, size in pieces
     ]
     parcels = weights[:3] + vectors + weights[3:]
@@ -214,9 +214,9 @@
 
     def pass_on():
         for k, buf, send_sem in (
-            (0, first_buf, weight_send.at[0]),
+            (0, weight_buf.at[:, pl.ds(0, split)], weight_send),
             (2, vector_buf, vector_send),
-            (1, second_buf, weight_send.at[1]),
+            (1, weight_buf.at[:, pl.ds(split, depth + block)], weight_send),
         ):
             for step in range(len(far)):
                 piece = buf.at[lax.rem(ch + chs - cores * (step + 1), chs)]
@@ -332,9 +332,9 @@
         scaled = (weight.astype(F32) * (0.5 * column)).astype(BF16)
         return fold(dot_nn, scaled, out_tails[u])
 
-    def parts_of(u, buf):
+    def parts_of(u, buf, at):
         weights = [
-            buf[:, part * block : (part + 1) * block, :].reshape(lanes, lanes)
+            buf[:, at + part * block : at + (part + 1) * block, :].reshape(lanes, lanes)
             for part in range(depth // block)
         ]
         return [
@@ -358,15 +358,15 @@
         return normed_product(product, statistics(values), folded)
 
     drain(last_gate_buf, gate_sem)
-    drain(first_buf.at[pl.ds(0, chs - len(far))], parcel_recv.at[0])
-    first_parts = parts_of(0, first_buf)
-    first_gate = fold_in(0, first_buf[:, depth : depth + block, :].reshape(lanes, lanes))
-    first_mix = fold_out(0, first_buf[:, depth + block :, :].reshape(lanes, lanes))
-    drain(second_buf.at[pl.ds(0, chs - len(far))], parcel_recv.at[1])
-    second_parts = parts_of(1, second_buf)
+    drain(weight_buf.at[pl.ds(0, chs - len(far)), pl.ds(0, split)], parcel_recv.at[0])
+    first_parts = parts_of(0, weight_buf, 0)
+    first_gate = fold_in(0, weight_buf[:, depth : depth + block, :].reshape(lanes, lanes))
+    first_mix = fold_out(0, weight_buf[:, depth + block : split, :].reshape(lanes, lanes))
+    drain(weight_buf.at[pl.ds(0, chs - len(far)), pl.ds(split, depth + block)], parcel_recv.at[1])
+    second_parts = parts_of(1, weight_buf, split)
     last_gate = fold_in(1, last_gate_buf[...])
     last_mix = fold_out(
-        1, dot_nt(second_buf[:, depth:, :].reshape(lanes, lanes), chosen).astype(BF16)
+        1, dot_nt(weight_buf[:, split + depth :, :].reshape(lanes, lanes), chosen).astype(BF16)
     )
 
     drain(block_buf, block_recv)
@@ -401,8 +401,7 @@
 
     drain(block_buf.at[pl.ds(0, rows * chs - 1)], block_send)
     drain(vector_buf.at[pl.ds(0, chs - 1)], vector_send)
-    drain(first_buf.at[pl.ds(0, chs - 1)], weight_send.at[0])
-    drain(second_buf.at[pl.ds(0, chs - 1)], weight_send.at[1])
+    drain(weight_buf.at[pl.ds(0, chs - 1)], weight_send)
 
 
 def window_body(
@@ -437,8 +436,7 @@
             pltpu.VMEM((2, layers, lanes), F32),
             pltpu.VMEM((n, block), BF16),
             pltpu.VMEM((rows * chs, n, block), BF16),
-            pltpu.VMEM((chs, (parts + 2) * block, lanes), BF16),
-            pltpu.VMEM((chs, (parts + 1) * block, lanes), BF16),
+            pltpu.VMEM((chs, (2 * parts + 3) * block, lanes), BF16),
             pltpu.VMEM((block, lanes), BF16),
             pltpu.VMEM((chs, 3, layers, block), F32),
             pltpu.VMEM((n * n, lanes), F32),
@@ -452,7 +450,7 @@
             dma,
             dma,
             dma,
-            dma((2,)),
+            dma,
             dma((3,)),
             dma((chs // 2 - 1, 3)),
             dma,

time: 10.3 us -> 10.3 us (level)
  no operation moved by 1% of the time
where the time goes in v7:
time: 10.3 us; the launch traced here: 10.1 us
  Pallas kernels  9.56 us (93%)
  local copies, waits for them, and re-layouts  0.58 us (6%)
    pallas_call x1, Pallas kernels, window_body(): pl.pallas_call(functools.partial(window_kernel, rows, chs), out_shape=plt...  9.56 us
    unnamed x1, local copies, waits for them, and re-layouts  0.58 us

profile of v7, /device:TPU:0, one launch (start us, length us, event | category | flops | bytes accessed | tf_op | source)
XLA Modules:
  0.0 10.1 jit_solution(7290243782930765413)
XLA Ops:
  0.0 9.6 %shard_map.109 = bf16[8,32]{1,0:T(8,128)(2,1)S(1)} custom-call(s32[8]{0:T(128)} %mask_hbm.1, s32[8]{0:T(128)} %chain_hbm.1, bf16[8,32]{1,0:T(8,128)(2,1)} %bitcast.13, f32[2,128]{1,0:T(2,128)} %in_gain_hbm.1, f32[2,128]{1,0:T(2,128)} %in_bias_hbm.1, bf16[2,128,128]{2,1,0:T(8,128)(2,1)} %bitcast.11, bf16[2,32,128]{2,1,0:T(8,128)(2,1)} %bitcast.12, ...), custom_call_target="tpu_custom_call" | custom-call | tf_op jit(solution)/shard_map/pallas_call | solution.py:428
  9.6 0.6 %copy.13 = bf16[32,1,8]{0,2,1:T(8,128)(2,1)} copy(bf16[32,1,8]{0,2,1:T(8,128)(2,1)S(1)} %bitcast.10) | data formatting | bytes 1024

commit v8 on v7

--- a/solution.py
+++ b/solution.py
@@ -108,12 +108,6 @@
         def _(other):
             greet(0, other)
 
-    for mate in mates:
-
-        @pl.when((mate > ch) & (row < last) & (here >= cores))
-        def _():
-            greet(row, mate)
-
     lower_mates = lax.rem(ch, cores) + ch // cores
     greeted_above = jnp.minimum(ch, cores) + jnp.where(ch < cores, 0, lower_mates - 1)
     greetings = jnp.where(
@@ -144,6 +138,12 @@
         @pl.when(here > m)
         def _():
             send_block(pair_hbm, 0, m)
+
+    for mate in mates:
+
+        @pl.when((mate > ch) & (row < last) & (here >= cores))
+        def _():
+            greet(row, mate)
 
     @pl.when(is_last)
     def _():

time: 10.3 us -> 10.3 us (level)
  no operation moved by 1% of the time
where the time goes in v8:
time: 10.3 us; the launch traced here: 10.1 us
  Pallas kernels  9.56 us (93%)
  local copies, waits for them, and re-layouts  0.58 us (6%)
    pallas_call x1, Pallas kernels, window_body(): pl.pallas_call(functools.partial(window_kernel, rows, chs), out_shape=plt...  9.56 us
    unnamed x1, local copies, waits for them, and re-layouts  0.58 us

profile of v8, /device:TPU:0, one launch (start us, length us, event | category | flops | bytes accessed | tf_op | source)
XLA Modules:
  0.0 10.1 jit_solution(2367019176833818292)
XLA Ops:
  0.0 9.6 %shard_map.109 = bf16[8,32]{1,0:T(8,128)(2,1)S(1)} custom-call(s32[8]{0:T(128)} %mask_hbm.1, s32[8]{0:T(128)} %chain_hbm.1, bf16[8,32]{1,0:T(8,128)(2,1)} %bitcast.13, f32[2,128]{1,0:T(2,128)} %in_gain_hbm.1, f32[2,128]{1,0:T(2,128)} %in_bias_hbm.1, bf16[2,128,128]{2,1,0:T(8,128)(2,1)} %bitcast.11, bf16[2,32,128]{2,1,0:T(8,128)(2,1)} %bitcast.12, ...), custom_call_target="tpu_custom_call" | custom-call | tf_op jit(solution)/shard_map/pallas_call | solution.py:428
  9.6 0.6 %copy.13 = bf16[32,1,8]{0,2,1:T(8,128)(2,1)} copy(bf16[32,1,8]{0,2,1:T(8,128)(2,1)S(1)} %bitcast.10) | data formatting | bytes 1024
